TPU v7x, 32 devices: a whole 2x2x4 slice. The times are simulated.
32 devices in a mesh: section: 4 (over y, x), seq: 8 (over z, core).
Axes of the slice: x: 2, y: 2, z: 4, core: 2. Of those that a mesh axis runs over, the one named last changes fastest.
Arguments:
- tokens: bfloat16 [4096, 2048], P('seq', 'section'), may hold values from -6 to 6
- norm_gain: float32 [2048], replicated, may hold values from 0.25 to 1.75
- w_query: bfloat16 [2048, 2048], P('seq', 'section'), may hold values from -0.3125 to 0.3125
- w_key: bfloat16 [2048, 512], P('seq', 'section'), may hold values from -0.125 to 0.125
- w_value: bfloat16 [2048, 512], P('seq', 'section'), may hold values from -0.125 to 0.125
- w_out: bfloat16 [2048, 2048], P('seq', 'section'), may hold values from -0.25 to 0.25
- router_gate: float32 [4096], P('seq'), may hold values from 0.25 to 1
- chosen_blocks: int32 [8, 1], replicated, may hold values from 0 to 3, as said below
- block_counts: int32 [8], replicated, may hold values from 0 to 1, as said below
Outputs:
- mixed: bfloat16 [4096, 2048], P('seq', 'section')
Inputs may be any that keep to these rules, and one draw needn't show every extreme that they name: `chosen_blocks`: in each segment's row the entries name distinct blocks of 128 rows of that segment, in increasing order; only the first block_counts entries are used. `block_counts`: some segment has one chosen block and some segment has none.
All inputs are finite; a program needn't handle non-finite values.
Results may differ from a plain program's by a relative error of at most 0.0034.
Values may be sent and summed in bfloat16 or wider, within the bound.
A program may use at most 64 MiB of HBM per device.

v0:
```python
import math

import jax
import jax.numpy as jnp
from jax import lax
from jax.sharding import PartitionSpec as P

HEADS = 16
KV_HEADS = 4
HEAD_DIM = 128
BLOCK = 128


EPSILON = 1e-05


def local(
    tokens, norm_gain, w_query, w_key, w_value, w_out, router_gate, chosen_blocks, block_counts
):
    seq_count = lax.axis_size("seq")
    my_index = lax.axis_index("seq")
    tok_rows = tokens.shape[0]
    capacity = chosen_blocks.shape[1] * BLOCK
    query_cols = w_query.shape[1]
    kv_cols = w_key.shape[1]
    kv_groups = kv_cols // HEAD_DIM
    repeat_count = HEADS // KV_HEADS
    head_groups = kv_groups * repeat_count
    score_scale = HEAD_DIM ** (-0.5)
    beyond = seq_count * tok_rows
    slot_index = jnp.arange(capacity, dtype=jnp.int32)
    local_all = (
        jnp.take(chosen_blocks, slot_index // BLOCK, axis=1) * BLOCK + (slot_index % BLOCK)[None, :]
    )
    place_all = jnp.arange(seq_count, dtype=jnp.int32)[:, None] * tok_rows + local_all
    live_all = (slot_index // BLOCK)[None, :] < block_counts[:, None]
    key_place_all = jnp.where(live_all, place_all, beyond).reshape(-1)
    my_rows = lax.dynamic_index_in_dim(local_all, my_index, 0, keepdims=False)
    my_places = lax.dynamic_index_in_dim(place_all, my_index, 0, keepdims=False)
    my_live = lax.dynamic_index_in_dim(live_all, my_index, 0, keepdims=False)
    picked = jnp.take(tokens, my_rows, axis=0)
    full_rows = lax.all_gather(picked, "section", axis=1, tiled=True)
    features = full_rows.astype(jnp.float32)
    normed = (
        features
        * lax.rsqrt(jnp.mean(features * features, axis=-1, keepdims=True) + EPSILON)
        * norm_gain
    ).astype(jnp.bfloat16)
    weight_pieces = (
        lax.all_gather(w_query, "seq", axis=0, tiled=True),
        lax.all_gather(w_key, "seq", axis=0, tiled=True),
        lax.all_gather(w_value, "seq", axis=0, tiled=True),
    )
    columns = normed
    query_sum, key_sum, value_sum = tuple(
        (
            jnp.dot(columns, weight_rows, preferred_element_type=jnp.float32)
            for weight_rows in weight_pieces
        )
    )
    queries = query_sum.astype(jnp.bfloat16)
    kv_panel = jnp.concatenate([key_sum, value_sum], axis=1).astype(jnp.bfloat16)

    def tile_terms(
        query_tile, query_places, lower_bound, upper_bound, key_tile, key_places, key_segments
    ):
        tile_rows = key_tile.shape[0]
        key_part = key_tile[:, :kv_cols].reshape(tile_rows, kv_groups, HEAD_DIM)
        value_part = key_tile[:, kv_cols:].reshape(tile_rows, kv_groups, HEAD_DIM)
        scores = (
            jnp.einsum("qgrd,kgd->grqk", query_tile, key_part, preferred_element_type=jnp.float32)
            * score_scale
        )
        in_range = (key_segments >= lower_bound) & (key_segments < upper_bound)
        allowed = (key_places[None, :] <= query_places[:, None]) & in_range[None, :]
        weights = jnp.where(allowed[None, None], jnp.exp(scores), 0.0)
        totals = jnp.sum(weights, axis=-1).reshape(head_groups, capacity)
        summed = jnp.einsum(
            "grqk,kgd->qgrd",
            weights.astype(jnp.bfloat16),
            value_part,
            preferred_element_type=jnp.float32,
        )
        return (summed.reshape(capacity, query_cols), totals)

    queries_heads = queries.reshape(capacity, kv_groups, repeat_count, HEAD_DIM)
    my_top = jnp.max(jnp.where(my_live, my_places, -1))
    query_sets = ((queries_heads, my_places, my_top, 0, seq_count),)
    empty_partials = tuple(
        (
            (
                jnp.zeros((capacity, query_cols), jnp.float32),
                jnp.zeros((head_groups, capacity), jnp.float32),
            )
            for unused_set in query_sets
        )
    )
    panel_piece = lax.all_gather(kv_panel, "seq", axis=0, tiled=True)
    piece_rows = panel_piece.shape[0]
    piece_segments = jnp.arange(piece_rows, dtype=jnp.int32) // capacity
    partials = empty_partials
    piece_rows = panel_piece.shape[0]
    tile_width = math.gcd(piece_rows, 1024)
    tile_count = piece_rows // tile_width
    tile_stack = (
        panel_piece.reshape(tile_count, tile_width, panel_piece.shape[1]),
        key_place_all.reshape(tile_count, tile_width),
        piece_segments.reshape(tile_count, tile_width),
    )

    def fold_tile(running, tile_data):
        key_tile, tile_places, tile_segments = tile_data
        updated = []
        for (numerator, denominator), (
            query_tile,
            query_places,
            query_top,
            lower_bound,
            upper_bound,
        ) in zip(running, query_sets):
            addition = tile_terms(
                query_tile,
                query_places,
                lower_bound,
                upper_bound,
                key_tile,
                tile_places,
                tile_segments,
            )
            updated.append((numerator + addition[0], denominator + addition[1]))
        return (tuple(updated), None)

    partials, unused = lax.scan(fold_tile, partials, tile_stack)
    own_numerator, own_denominator = partials[0]
    safe_denominator = jnp.where(my_live[None, :], own_denominator, 1.0)
    attended = (
        (
            own_numerator.reshape(capacity, head_groups, HEAD_DIM)
            / jnp.transpose(safe_denominator)[:, :, None]
        )
        .reshape(capacity, query_cols)
        .astype(jnp.bfloat16)
    )
    all_heads = lax.all_gather(attended, "section", axis=1, tiled=True)
    columns = all_heads
    update = jnp.dot(
        columns,
        lax.all_gather(w_out, "seq", axis=0, tiled=True),
        preferred_element_type=jnp.float32,
    )
    gate_rows = jnp.take(router_gate, my_rows)
    new_rows = (picked.astype(jnp.float32) + gate_rows[:, None] * update).astype(jnp.bfloat16)
    targets = jnp.where(my_live, my_rows, tok_rows)
    return tokens.at[targets].set(new_rows, mode="drop")


def solution(mesh):
    return jax.shard_map(
        local,
        mesh=mesh,
        in_specs=(
            P("seq", "section"),
            P(),
            P("seq", "section"),
            P("seq", "section"),
            P("seq", "section"),
            P("seq", "section"),
            P("seq"),
            P(),
            P(),
        ),
        out_specs=P("seq", "section"),
        check_vma=False,
    )
```

profile of v0, /device:TPU:0, one launch (start us, length us, event | category | flops | bytes accessed | tf_op | source)
XLA Modules:
  0.0 103.4 jit_solution(16189843208291968105)
XLA Ops:
  6.5 0.0 copy-start
  6.5 0.0 all-gather.3.cloned.1.call-start
  6.5 1.1 %copy.28 = bf16[512,512]{1,0:T(8,128)(2,1)S(1)} copy(bf16[512,512]{1,0:T(8,128)(2,1)} %param.9) | data formatting | bytes 1048576
  7.6 0.0 all-gather.3.cloned.1.call-update
  7.6 0.0 copy-start.3
  7.6 0.0 all-gather.5.cloned.1.call-start
  7.7 0.7 all-gather.5.cloned.1.call-update
  8.4 0.7 broadcast_compare_fusion
  9.2 0.7 select_bitcast_fusion
  9.9 0.0 copy-start.4
  9.9 0.8 gather_fusion
  10.8 0.0 copy-done
  10.8 1.3 %gather_fusion.1 = f32[128]{0:T(128)S(1)} fusion(f32[512]{0:T(512)S(1)} %copy-done, s32[1024]{0:T(1024)S(1)} %pad_clamp_fusion), kind=kCustom, calls=%fused_computation.1 | custom fusion | bytes 1536 | tf_op jit(solution)/shard_map/jit(_take)/gather | solution.py:151
  12.1 0.1 broadcast_select_fusion
  12.2 11.5 %all_gather.21 = bf16[128,2048]{1,0:T(8,128)(2,1)S(1)} all-gather(bf16[128,512]{1,0:T(8,128)(2,1)S(1)} %broadcast_select_fusion), channel_id=1, replica_groups=mesh['section'=4,'seq'=8] {'section'}, dimensions={1}, use_global_device_ids=true | all-gather | bytes 655360 | tf_op jit(solution)/shard_map/all_gather | solution.py:42
  23.7 0.2 fusion.5
  23.9 0.0 copy-done.2
  24.0 17.8 %all_gather.23 = bf16[2048,128]{1,0:T(8,128)(2,1)S(1)} all-gather(bf16[256,128]{1,0:T(8,128)(2,1)S(1)} %copy-done.2), channel_id=1, replica_groups=mesh['section'=4,'seq'=8] {'seq'}, dimensions={0}, use_global_device_ids=true | all-gather | bytes 589824 | tf_op jit(solution)/shard_map/all_gather | solution.py:52
  41.8 0.0 copy-done.1
  41.8 0.0 copy-done.3
  41.8 14.8 %all_gather.22 = bf16[2048,128]{1,0:T(8,128)(2,1)S(1)} all-gather(bf16[256,128]{1,0:T(8,128)(2,1)S(1)} %copy-done.3), channel_id=1, replica_groups=mesh['section'=4,'seq'=8] {'seq'}, dimensions={0}, use_global_device_ids=true | all-gather | bytes 589824 | tf_op jit(solution)/shard_map/all_gather | solution.py:51
  56.5 0.0 copy-done.4
  56.6 0.4 convolution_convert_fusion.1
  57.0 0.4 convolution_convert_fusion.2
  57.4 0.3 compare_and_fusion
  57.7 20.5 %all_gather.24 = bf16[1024,256]{0,1:T(8,128)(2,1)S(1)} all-gather(bf16[128,256]{0,1:T(8,128)(2,1)S(1)} %pad_maximum_fusion), channel_id=1, replica_groups=mesh['section'=4,'seq'=8] {'seq'}, dimensions={0}, use_global_device_ids=true | all-gather | bytes 589824 | tf_op jit(solution)/shard_map/all_gather | solution.py:98
  78.3 2.1 %fusion.4 = bf16[16,4,8,128]{3,2,1,0:T(8,128)(2,1)S(1)} fusion(bf16[2048,512]{1,0:T(8,128)(2,1)} %all-gather.3.cloned.1.call-done, bf16[128,2048]{1,0:T(8,128)(2,1)S(1)} %all_gather.21, f32[2048]{0:T(1024)S(1)} %copy-done.4, f32[128]{0:T(128)S(1)} %add_rsqrt_fusion), kind=kOutput, calls=%fused_computation.12 | convolution fusion | flops 269549568 | bytes 2761216 | tf_op jit(solution)/shard_map/dot_general | solution.py:57
  80.4 0.6 fusion
  81.0 0.5 fusion.9
  81.5 10.0 %all_gather.26 = bf16[128,2048]{0,1:T(8,128)(2,1)S(1)} all-gather(bf16[128,512]{0,1:T(8,128)(2,1)S(1)} %fusion.15), channel_id=1, replica_groups=mesh['section'=4,'seq'=8] {'section'}, dimensions={1}, use_global_device_ids=true | all-gather | bytes 655360 | tf_op jit(solution)/shard_map/all_gather | solution.py:144
  91.5 2.1 %fusion.3 = bf16[128,512]{1,0:T(8,128)(2,1)S(1)} fusion(bf16[128,2048]{0,1:T(8,128)(2,1)S(1)} %all_gather.26, bf16[2048,512]{1,0:T(8,128)(2,1)} %all-gather.5.cloned.1.call-done, bf16[128,512]{1,0:T(8,128)(2,1)S(1)} %broadcast_select_fusion, f32[128]{0:T(128)S(1)} %get-tuple-element.19), kind=kOutput, calls=%fused_computation.10 | convolution fusion | flops 268697600 | bytes 2884096 | tf_op jit(solution)/shard_map/dot_general | solution.py:146
  93.6 2.9 %scatter_fusion = bf16[512,512]{1,0:T(8,128)(2,1)} fusion(bf16[512,512]{1,0:T(8,128)(2,1)} %copy-done.1, s32[128]{0:T(128)S(1)} %get-tuple-element.22, bf16[128,512]{1,0:T(8,128)(2,1)S(1)} %fusion.3), kind=kCustom, calls=%fused_computation.2 | custom fusion | bytes 393728 | tf_op jit(solution)/shard_map/scatter | solution.py:154
  (17 shorter events, 0.1 us)
Async XLA Ops:
  6.5 4.3 %copy-start = (f32[512]{0:T(512)S(1)}, f32[512]{0:T(512)}, u32[]{:S(2)}) copy-start(f32[512]{0:T(512)} %param.15) | copy-start | bytes 6148
  6.5 71.7 %all-gather.3.cloned.1.call-start = ((), (), s32[]{:S(2)}) async-start(), calls=%async_computation | async-start | bytes 2359296 | tf_op jit(solution)/shard_map/all_gather | solution.py:50
  7.6 34.2 %copy-start.1 = (bf16[512,512]{1,0:T(8,128)(2,1)}, bf16[512,512]{1,0:T(8,128)(2,1)S(1)}, u32[]{:S(2)}) copy-start(bf16[512,512]{1,0:T(8,128)(2,1)S(1)} %copy.28) | copy-start | bytes 1572868
  7.6 16.4 %copy-start.2 = (bf16[256,128]{1,0:T(8,128)(2,1)S(1)}, bf16[256,128]{1,0:T(8,128)(2,1)}, u32[]{:S(2)}) copy-start(bf16[256,128]{1,0:T(8,128)(2,1)} %param.13) | copy-start | bytes 196612
  7.6 34.2 %copy-start.3 = (bf16[256,128]{1,0:T(8,128)(2,1)S(1)}, bf16[256,128]{1,0:T(8,128)(2,1)}, u32[]{:S(2)}) copy-start(bf16[256,128]{1,0:T(8,128)(2,1)} %param.12) | copy-start | bytes 196612
  7.6 83.9 %all-gather.5.cloned.1.call-start = ((), (), s32[]{:S(2)}) async-start(), calls=%async_computation.1 | async-start | bytes 2359296 | tf_op jit(solution)/shard_map/all_gather | solution.py:148
  9.9 46.6 %copy-start.4 = (f32[2048]{0:T(1024)S(1)}, f32[2048]{0:T(1024)}, u32[]{:S(2)}) copy-start(f32[2048]{0:T(1024)} %param.10) | copy-start | bytes 24580
Sparse Core Ops, SparseCore 0:
  8.9 36.0 all-gather.2
  46.7 32.7 all-gather.4
where the time goes:
time: 104 us; the launch traced here: 103 us
  blocking collectives  74.6 us (72%)
  between operations  13.6 us (13%)
  local copies, waits for them, and re-layouts  6.14 us (6%)
  matrix products  6.09 us (6%)
  other arithmetic  2.19 us (2%)
    all_gather x1, blocking collectives, local(): panel_piece = lax.all_gather(kv_panel, 'seq', axis=0, tiled=True)  20.5 us
    all_gather x1, blocking collectives, local(): lax.all_gather(w_value, 'seq', axis=0, tiled=True)  17.8 us
    all_gather x1, blocking collectives, local(): lax.all_gather(w_key, 'seq', axis=0, tiled=True)  14.8 us
    all_gather x1, blocking collectives, local(): full_rows = lax.all_gather(picked, 'section', axis=1, tiled=True)  11.5 us
    all_gather x1, blocking collectives, local(): all_heads = lax.all_gather(attended, 'section', axis=1, tiled=True)  9.97 us
    scatter x1, local copies, waits for them, and re-layouts, local(): return tokens.at[targets].set(new_rows, mode='drop')  2.93 us
    dot_general x3, matrix products, local(): jnp.dot(columns, weight_rows, preferred_element_type=jnp.float32)  2.93 us
    dot_general x1, matrix products, local(): jnp.dot(columns, lax.all_gather(w_out, 'seq', axis=0, tiled=True), prefer...  2.08 us
  transfers between devices with their start and end apart: 2, of which 0 were waited for; matrix products, arithmetic and copies ran while one was open for 8% of the time, Pallas kernels for 0%

commit v1 on v0

v1 whole, which is shorter than its diff:
```python
import functools
import math

import jax
import jax.numpy as jnp
from jax import lax
from jax.experimental import pallas as pl
from jax.experimental.pallas import tpu as pltpu
from jax.sharding import PartitionSpec as P

HEADS = 16
KV_HEADS = 4
HEAD_DIM = 128
BLOCK = 128
EPSILON = 1e-05
MESH = pl.DeviceIdType.MESH

KEY, VALUE, QUERY_A, QUERY_B, PANEL, OUT_A, OUT_B = range(7)


def repeat(low, high, body):
    if high - low <= 4:
        for step in range(low, high):
            body(step)
    elif high > low:

        def wrapped(step, carry):
            body(step)
            return carry

        lax.fori_loop(low, high, wrapped, 0)


def kernel(
    seq_count,
    section_count,
    picked_ref,
    gain_ref,
    gate_ref,
    place_ref,
    live_ref,
    key_place_ref,
    wq_in,
    wk_in,
    wv_in,
    wo_in,
    out_ref,
    rows_all,
    normed_ref,
    wk,
    wv,
    wq,
    wo,
    panel,
    queries_ref,
    numer_ref,
    denom_ref,
    heads_all,
    recv,
    send_up,
    send_down,
    send_pair,
    own_sem,
    rows_send,
    rows_recv,
    heads_send,
    heads_recv,
):
    me = lax.axis_index("seq")
    section = lax.axis_index("section")
    line = seq_count // 2
    spot = me // 2
    core = lax.rem(me, 2)
    pair = spot * 2 + 1 - core
    capacity, width = picked_ref.shape
    kv_cols = wk_in.shape[1]
    groups = kv_cols // HEAD_DIM
    ratio = HEADS // KV_HEADS
    half_q = wq_in.shape[1] // 2
    half_o = wo_in.shape[1] // 2
    depth = section_count * width

    def rows_of(block, size):
        return pl.ds(pl.multiple_of(block * size, size), size)

    def full(chunk, block):
        if chunk == KEY:
            return wk.at[rows_of(block, wk_in.shape[0]), :]
        if chunk == VALUE:
            return wv.at[rows_of(block, wv_in.shape[0]), :]
        if chunk in (QUERY_A, QUERY_B):
            return wq.at[chunk - QUERY_A, rows_of(block, wq_in.shape[0]), :]
        if chunk == PANEL:
            return panel.at[rows_of(block, capacity), :]
        return wo.at[chunk - OUT_A, rows_of(block, wo_in.shape[0]), :]

    def own(chunk):
        if chunk == KEY:
            return wk_in
        if chunk == VALUE:
            return wv_in
        if chunk in (QUERY_A, QUERY_B):
            return wq_in.at[:, pl.ds((chunk - QUERY_A) * half_q, half_q)]
        if chunk == PANEL:
            return full(PANEL, me)
        return wo_in.at[:, pl.ds((chunk - OUT_A) * half_o, half_o)]

    def transfer(chunk, source, sems, target, mine):
        block = source * 2 + core
        return pltpu.make_async_remote_copy(
            src_ref=own(chunk) if mine else full(chunk, block),
            dst_ref=full(chunk, block),
            send_sem=sems.at[chunk, source],
            recv_sem=recv.at[chunk, block],
            device_id={"seq": target},
            device_id_type=MESH,
        )

    def await_block(chunk, block):
        pltpu.make_async_remote_copy(
            src_ref=full(chunk, block),
            dst_ref=full(chunk, block),
            send_sem=send_pair.at[chunk, 0],
            recv_sem=recv.at[chunk, block],
            device_id={"seq": pair},
            device_id_type=MESH,
        ).wait_recv()

    def begin(chunk):
        @pl.when(spot + 1 < line)
        def _():
            transfer(chunk, spot, send_up, me + 2, True).start()

        @pl.when(spot > 0)
        def _():
            transfer(chunk, spot, send_down, me - 2, True).start()

        transfer(chunk, spot, send_pair, pair, True).start()

    def relay(chunk, step):
        @pl.when(spot - step >= 0)
        def _():
            source = spot - step
            await_block(chunk, source * 2 + core)

            @pl.when(spot + 1 < line)
            def _():
                transfer(chunk, source, send_up, me + 2, False).start()

            transfer(chunk, source, send_pair, pair, False).start()

        @pl.when(spot + step < line)
        def _():
            source = spot + step
            await_block(chunk, source * 2 + core)

            @pl.when(spot > 0)
            def _():
                transfer(chunk, source, send_down, me - 2, False).start()

            transfer(chunk, source, send_pair, pair, False).start()

    def relay_all(chunks, low, high):
        def body(step):
            for chunk in chunks:
                relay(chunk, step)

        repeat(low, high, body)

    def await_pair(chunk):
        repeat(0, line, lambda source: await_block(chunk, source * 2 + 1 - core))

    def finish_sends(chunk):
        def body(source):
            @pl.when((spot + 1 < line) & (source <= spot))
            def _():
                transfer(chunk, source, send_up, me + 2, False).wait_send()

            @pl.when((spot > 0) & (source >= spot))
            def _():
                transfer(chunk, source, send_down, me - 2, False).wait_send()

            transfer(chunk, source, send_pair, pair, False).wait_send()

        repeat(0, line, body)

    def own_copy(chunk):
        return pltpu.make_async_copy(own(chunk), full(chunk, me), own_sem.at[chunk])

    def spread(source, target, send, receive, offset):
        peer = lax.rem(section + offset, section_count)
        return pltpu.make_async_remote_copy(
            src_ref=source,
            dst_ref=target.at[section],
            send_sem=send.at[offset],
            recv_sem=receive.at[section],
            device_id={"section": peer},
            device_id_type=MESH,
        )

    def await_spread(target, send, receive, offset):
        peer = lax.rem(section + offset, section_count)
        pltpu.make_async_remote_copy(
            src_ref=target.at[peer],
            dst_ref=target.at[peer],
            send_sem=send.at[offset],
            recv_sem=receive.at[peer],
            device_id={"section": peer},
            device_id_type=MESH,
        ).wait_recv()

    barrier = pltpu.get_barrier_semaphore()

    @pl.when(spot + 1 < line)
    def _():
        pl.semaphore_signal(barrier, inc=1, device_id={"seq": me + 2}, device_id_type=MESH)

    @pl.when(spot > 0)
    def _():
        pl.semaphore_signal(barrier, inc=1, device_id={"seq": me - 2}, device_id_type=MESH)

    pl.semaphore_signal(barrier, inc=1, device_id={"seq": pair}, device_id_type=MESH)
    for offset in range(1, section_count):
        peer = lax.rem(section + offset, section_count)
        pl.semaphore_signal(barrier, inc=1, device_id={"section": peer}, device_id_type=MESH)
    neighbours = jnp.where(spot + 1 < line, 1, 0) + jnp.where(spot > 0, 1, 0)
    pl.semaphore_wait(barrier, section_count + neighbours)

    begin(KEY)
    begin(VALUE)
    for offset in range(1, section_count):
        spread(picked_ref, rows_all, rows_send, rows_recv, offset).start()
    for chunk in (KEY, VALUE, QUERY_A, QUERY_B, OUT_A, OUT_B):
        own_copy(chunk).start()
    rows_all[section] = picked_ref[...]
    relay_all((KEY, VALUE), 1, line - 1)
    begin(QUERY_A)
    begin(QUERY_B)
    for offset in range(1, section_count):
        await_spread(rows_all, rows_send, rows_recv, offset)
    square_sum = jnp.zeros((capacity, 1), jnp.float32)
    for part in range(section_count):
        features = rows_all[part].astype(jnp.float32)
        square_sum += jnp.sum(features * features, axis=-1, keepdims=True)
    factor = lax.rsqrt(square_sum / depth + EPSILON)
    for part in range(section_count):
        cols = pl.ds(part * width, width)
        normed_ref[:, cols] = (
            rows_all[part].astype(jnp.float32) * factor * gain_ref[:, cols]
        ).astype(jnp.bfloat16)
    relay_all((KEY, VALUE), max(line - 1, 1), line)
    for chunk in (KEY, VALUE):
        await_pair(chunk)
        own_copy(chunk).wait()
    normed = normed_ref[...]
    my_rows = rows_of(me, capacity)
    panel[my_rows, pl.ds(0, kv_cols)] = jnp.dot(
        normed, wk[...], preferred_element_type=jnp.float32
    ).astype(jnp.bfloat16)
    panel[my_rows, pl.ds(kv_cols, kv_cols)] = jnp.dot(
        normed, wv[...], preferred_element_type=jnp.float32
    ).astype(jnp.bfloat16)
    begin(PANEL)
    relay_all((QUERY_A, QUERY_B, PANEL), 1, line - 1)
    begin(OUT_A)
    begin(OUT_B)
    relay_all((QUERY_A, QUERY_B, PANEL), max(line - 1, 1), line)
    heads_half = half_q // HEAD_DIM
    for half in range(2):
        await_pair(QUERY_A + half)
        own_copy(QUERY_A + half).wait()
        sums = jnp.dot(normed_ref[...], wq[half], preferred_element_type=jnp.float32)
        for head in range(heads_half):
            queries_ref[half * heads_half + head] = sums[
                :, head * HEAD_DIM : (head + 1) * HEAD_DIM
            ].astype(jnp.bfloat16)
    await_pair(PANEL)
    scale = HEAD_DIM ** (-0.5)
    tiles, tile = key_place_ref.shape
    places = jnp.concatenate([place_ref[...]] * ratio, axis=0)
    live = jnp.concatenate([live_ref[...]] * ratio, axis=0)
    for group in range(groups):
        numer_ref[...] = jnp.zeros_like(numer_ref)
        denom_ref[...] = jnp.zeros_like(denom_ref)

        def fold(index):
            rows = pl.ds(index * tile, tile)
            keys = panel[rows, pl.ds(group * HEAD_DIM, HEAD_DIM)]
            values = panel[rows, pl.ds(kv_cols + group * HEAD_DIM, HEAD_DIM)]
            wide = queries_ref[pl.ds(group * ratio, ratio)].reshape(ratio * capacity, HEAD_DIM)
            scores = (
                lax.dot_general(
                    wide, keys, (((1,), (1,)), ((), ())), preferred_element_type=jnp.float32
                )
                * scale
            )
            allowed = key_place_ref[pl.ds(index, 1), :] <= places
            weights = jnp.where(allowed, jnp.exp(scores), 0.0)
            denom_ref[...] += jnp.sum(weights, axis=-1, keepdims=True)
            numer_ref[...] += jnp.dot(
                weights.astype(jnp.bfloat16), values, preferred_element_type=jnp.float32
            )

        repeat(0, tiles, fold)
        safe = jnp.where(live > 0, denom_ref[...], 1.0)
        result = (numer_ref[...] / safe).astype(jnp.bfloat16)
        for head in range(ratio):
            cols = pl.ds((group * ratio + head) * HEAD_DIM, HEAD_DIM)
            heads_all[section, :, cols] = result[head * capacity : (head + 1) * capacity]
    for offset in range(1, section_count):
        spread(heads_all.at[section], heads_all, heads_send, heads_recv, offset).start()
    relay_all((OUT_A, OUT_B), 1, line)
    for offset in range(1, section_count):
        await_spread(heads_all, heads_send, heads_recv, offset)
    head_cols = heads_all.shape[2]
    for half in range(2):
        await_pair(OUT_A + half)
        own_copy(OUT_A + half).wait()
        update = jnp.zeros((capacity, half_o), jnp.float32)
        for part in range(section_count):
            update += jnp.dot(
                heads_all[part],
                wo[half, pl.ds(part * head_cols, head_cols), :],
                preferred_element_type=jnp.float32,
            )
        cols = pl.ds(half * half_o, half_o)
        out_ref[:, cols] = (
            picked_ref[:, cols].astype(jnp.float32) + gate_ref[...] * update
        ).astype(out_ref.dtype)
    for chunk in range(7):
        finish_sends(chunk)
    for offset in range(1, section_count):
        spread(picked_ref, rows_all, rows_send, rows_recv, offset).wait_send()
        spread(heads_all.at[section], heads_all, heads_send, heads_recv, offset).wait_send()


def local(
    tokens, norm_gain, w_query, w_key, w_value, w_out, router_gate, chosen_blocks, block_counts
):
    seq_count = lax.axis_size("seq")
    section_count = lax.axis_size("section")
    me = lax.axis_index("seq")
    tok_rows, width = tokens.shape
    slots = chosen_blocks.shape[1]
    capacity = slots * BLOCK
    beyond = seq_count * tok_rows
    depth = section_count * width
    query_cols = w_query.shape[1]
    kv_cols = w_key.shape[1]
    ratio = HEADS // KV_HEADS
    line = seq_count // 2

    within = jnp.arange(BLOCK, dtype=jnp.int32)
    place_all = (
        jnp.arange(seq_count, dtype=jnp.int32)[:, None, None] * tok_rows
        + chosen_blocks[:, :, None] * BLOCK
        + within[None, None, :]
    )
    live_all = (
        jnp.arange(slots, dtype=jnp.int32)[None, :, None] < block_counts[:, None, None]
    )
    key_place = jnp.where(live_all, place_all, beyond).reshape(-1)
    tile = math.gcd(key_place.shape[0], 512)
    key_place = key_place.reshape(-1, tile)

    my_blocks = lax.dynamic_index_in_dim(chosen_blocks, me, 0, keepdims=False)
    my_count = lax.dynamic_index_in_dim(block_counts, me, 0, keepdims=False)
    starts = [my_blocks[slot] * BLOCK for slot in range(slots)]
    picked = jnp.concatenate(
        [lax.dynamic_slice_in_dim(tokens, start, BLOCK, 0) for start in starts], axis=0
    )
    gates = jnp.concatenate(
        [lax.dynamic_slice_in_dim(router_gate, start, BLOCK, 0) for start in starts], axis=0
    )
    my_places = jnp.concatenate([me * tok_rows + start + within for start in starts])
    my_live = (jnp.arange(capacity, dtype=jnp.int32) // BLOCK < my_count).astype(jnp.int32)

    vmem = pl.BlockSpec(memory_space=pltpu.VMEM)
    anywhere = pl.BlockSpec(memory_space=pl.ANY)
    bf16 = jnp.bfloat16
    dma = pltpu.SemaphoreType.DMA
    new_rows = pl.pallas_call(
        functools.partial(kernel, seq_count, section_count),
        out_shape=jax.ShapeDtypeStruct((capacity, width), tokens.dtype),
        in_specs=[vmem] * 6 + [anywhere] * 4,
        out_specs=vmem,
        scratch_shapes=[
            pltpu.VMEM((section_count, capacity, width), bf16),
            pltpu.VMEM((capacity, depth), bf16),
            pltpu.VMEM((depth, kv_cols), bf16),
            pltpu.VMEM((depth, kv_cols), bf16),
            pltpu.VMEM((2, depth, query_cols // 2), bf16),
            pltpu.VMEM((2, w_out.shape[0] * seq_count, w_out.shape[1] // 2), bf16),
            pltpu.VMEM((seq_count * capacity, 2 * kv_cols), bf16),
            pltpu.VMEM((query_cols // HEAD_DIM, capacity, HEAD_DIM), bf16),
            pltpu.VMEM((ratio * capacity, HEAD_DIM), jnp.float32),
            pltpu.VMEM((ratio * capacity, 1), jnp.float32),
            pltpu.VMEM((section_count, capacity, query_cols), bf16),
            dma((7, seq_count)),
            dma((7, line)),
            dma((7, line)),
            dma((7, line)),
            dma((7,)),
            dma((section_count,)),
            dma((section_count,)),
            dma((section_count,)),
            dma((section_count,)),
        ],
        compiler_params=pltpu.CompilerParams(collective_id=0, has_side_effects=True),
    )(
        picked,
        norm_gain[None, :],
        gates[:, None],
        my_places[:, None],
        my_live[:, None],
        key_place,
        w_query,
        w_key,
        w_value,
        w_out,
    )
    mixed = tokens
    for slot, start in enumerate(starts):
        part = slice(slot * BLOCK, (slot + 1) * BLOCK)
        chosen = jnp.where(slot < my_count, new_rows[part], picked[part])
        mixed = lax.dynamic_update_slice_in_dim(mixed, chosen, start, 0)
    return mixed


def solution(mesh):
    return jax.shard_map(
        local,
        mesh=mesh,
        in_specs=(
            P("seq", "section"),
            P(),
            P("seq", "section"),
            P("seq", "section"),
            P("seq", "section"),
            P("seq", "section"),
            P("seq"),
            P(),
            P(),
        ),
        out_specs=P("seq", "section"),
        check_vma=False,
    )
```

time: 104 us -> 69.9 us (0.67)
  blocking collectives: 74.6 us -> 0 us
  Pallas kernels: 0 us -> 57.6 us
  between operations: 13.6 us -> 3.14 us
  matrix products: 6.09 us -> 0 us
  other arithmetic: 2.19 us -> 4.2 us
  local copies, waits for them, and re-layouts: 6.14 us -> 4.43 us
    all_gather x5 -> x0, blocking collectives: 74.6 us -> none  [the longest x1 20.5 us: local(): panel_piece = lax.all_gather(kv_panel, 'seq', axis=0, tiled=True)]
    pallas_call x0 -> x1, Pallas kernels: none -> 57.6 us  [local(): pl.pallas_call(functools.partial(kernel, seq_count, section_count), out_s...]
    dot_general x6 -> x0, matrix products: 6.09 us -> none  [the longest x3 2.93 us: local(): jnp.dot(columns, weight_rows, preferred_element_type=jnp.float32)]
    scatter x1 -> x0, local copies, waits for them, and re-layouts: 2.93 us -> none  [local(): return tokens.at[targets].set(new_rows, mode='drop')]
    gather x2 -> x0, local copies, waits for them, and re-layouts: 2.12 us -> none  [the longest x1 1.27 us: local(): gate_rows = jnp.take(router_gate, my_rows)]
    dynamic_update_slice x0 -> x1, other arithmetic: none -> 1.66 us  [local(): mixed = lax.dynamic_update_slice_in_dim(mixed, chosen, start, 0)]
    dynamic_slice x0 -> x2, local copies, waits for them, and re-layouts: none -> 1.26 us  [the longest x1 0.65 us: local(): lax.dynamic_slice_in_dim(tokens, start, BLOCK, 0)]
    convert_element_type x1, other arithmetic: 0.03 us -> 1.24 us  [local(): (jnp.arange(capacity, dtype=jnp.int32) // BLOCK < my_count).astype(jnp.in...]
  transfers between devices with their start and end apart: 2 -> 0, of which waited for: 0 -> 0; matrix products, arithmetic and copies ran while one was open for 8% -> 0% of each run, Pallas kernels for 0% -> 0%
where the time goes in v1:
time: 69.9 us; the launch traced here: 69.3 us
  Pallas kernels  57.6 us (82%)
  local copies, waits for them, and re-layouts  4.43 us (6%)
  other arithmetic  4.2 us (6%)
  between operations  3.14 us (4%)
    pallas_call x1, Pallas kernels, local(): pl.pallas_call(functools.partial(kernel, seq_count, section_count), out_s...  57.6 us
    unnamed x9, local copies, waits for them, and re-layouts  1.74 us
    dynamic_update_slice x1, other arithmetic, local(): mixed = lax.dynamic_update_slice_in_dim(mixed, chosen, start, 0)  1.66 us

profile of v1, /device:TPU:0, one launch (start us, length us, event | category | flops | bytes accessed | tf_op | source)
XLA Modules:
  0.0 69.3 jit_solution(13545095053563456321)
XLA Ops:
  0.0 0.0 copy-start
  0.0 1.1 %copy.13 = bf16[512,512]{1,0:T(8,128)(2,1)S(1)} copy(bf16[512,512]{1,0:T(8,128)(2,1)} %param.9) | data formatting | bytes 1048576
  1.1 0.0 copy-start.1
  1.1 0.0 copy-start.3
  1.1 0.7 copy-done.3
  1.7 0.6 dynamic_slice.14
  2.3 0.0 copy-start.2
  3.0 0.0 copy-done.2
  3.0 0.6 fusion.5
  6.1 0.0 copy-done
  6.1 0.1 dynamic-slice_bitcast_fusion
  6.2 0.1 add_select_fusion.1
  6.2 0.6 select_n.46.key_place_ref
  6.8 0.7 %copy.10.gate_ref = f32[128,1]{1,0:T(8,128)} copy(f32[128,1]{0,1:T(1,128)S(1)} %dynamic-slice_bitcast_fusion) | data formatting | bytes 1024 | tf_op jit(solution)/shard_map/broadcast_in_dim | solution.py:413
  7.6 0.6 iota_add_fusion.place_ref
  8.2 1.2 %fusion.4.live_ref = s32[128,1]{1,0:T(8,128)} fusion(s32[]{:T(128)} %bitcast), kind=kLoop, calls=%fused_computation.10 | loop fusion | flops 1280 | bytes 516 | tf_op jit(solution)/shard_map/convert_element_type | solution.py:376
  9.4 0.7 constant_dynamic-slice_fusion.picked_ref
  10.1 57.6 %shard_map.91 = bf16[128,512]{1,0:T(8,128)(2,1)} custom-call(bf16[128,512]{1,0:T(8,128)(2,1)} %constant_dynamic-slice_fusion.picked_ref, f32[1,2048]{1,0:T(1,128)} %bitcast.11, f32[128,1]{1,0:T(8,128)} %copy.10.gate_ref, s32[128,1]{1,0:T(8,128)} %iota_add_fusion.place_ref, s32[128,1]{1,0:T(8,128)} %fusion.4.live_ref, s32[2,512]{1,0:T(2,128)} %select_n.46.key_place_ref, ...), custom_call_target="tpu_custom_call" | custom-call | tf_op jit(solution)/shard_map/pallas_call | solution.py:382
  67.7 0.0 copy-done.1
  67.7 1.7 %select_dynamic-update-slice_fusion = bf16[512,512]{1,0:T(8,128)(2,1)} fusion(bf16[512,512]{1,0:T(8,128)(2,1)} %copy-done.1, s32[]{:T(128)S(6)} %select_n.43, bf16[128,512]{1,0:T(8,128)(2,1)} %shard_map.91, pred[]{:T(512)S(6)} %gt.3), kind=kLoop, calls=%fused_computation | loop fusion | flops 65536 | bytes 393221 | tf_op jit(solution)/shard_map/dynamic_update_slice | solution.py:426
  (2 shorter events, 0.0 us)
Async XLA Ops:
  0.0 6.1 %copy-start = (f32[512]{0:T(512)S(1)}, f32[512]{0:T(512)}, u32[]{:S(2)}) copy-start(f32[512]{0:T(512)} %param.15) | copy-start | bytes 6148
  1.1 66.6 %copy-start.1 = (bf16[512,512]{1,0:T(8,128)(2,1)}, bf16[512,512]{1,0:T(8,128)(2,1)S(1)}, u32[]{:S(2)}) copy-start(bf16[512,512]{1,0:T(8,128)(2,1)S(1)} %copy.13) | copy-start | bytes 1572868
  1.1 0.7 copy-start.3
  2.3 0.7 copy-start.2

commit v2 on v1

v2 whole, which is shorter than its diff:
```python
import functools
import math

import jax
import jax.numpy as jnp
from jax import lax
from jax.experimental import pallas as pl
from jax.experimental.pallas import tpu as pltpu
from jax.sharding import PartitionSpec as P

HEADS = 16
KV_HEADS = 4
HEAD_DIM = 128
BLOCK = 128
EPSILON = 1e-05
MESH = pl.DeviceIdType.MESH

KEY, VALUE, QUERY_A, QUERY_B, OUT_A, OUT_B, PANEL, GUEST_PANEL = range(8)


def repeat(low, high, body):
    if high - low <= 4:
        for step in range(low, high):
            body(step)
    elif high > low:

        def wrapped(step, carry):
            body(step)
            return carry

        lax.fori_loop(low, high, wrapped, 0)


def kernel(
    seq_count,
    section_count,
    picked_ref,
    gain_ref,
    gate_ref,
    key_slot_ref,
    wq_in,
    wk_in,
    wv_in,
    wo_in,
    out_ref,
    rows_all,
    gate_rows,
    normed_ref,
    wk,
    wv,
    wq,
    wo,
    panel,
    queries_ref,
    numer_ref,
    denom_ref,
    heads_all,
    results,
    returned,
    recv,
    send_line,
    send_pair,
    own_sem,
    rows_send,
    rows_recv,
    heads_send,
    heads_recv,
    guest_send,
    guest_recv,
    back_send,
    back_recv,
):
    me = lax.axis_index("seq")
    section = lax.axis_index("section")
    line = seq_count // 2
    spot = me // 2
    core = lax.rem(me, 2)
    pair = spot * 2 + 1 - core
    slots = gate_ref.shape[0]
    capacity, width = out_ref.shape
    kv_cols = wk_in.shape[1]
    groups = kv_cols // HEAD_DIM
    ratio = HEADS // KV_HEADS
    half_q = wq_in.shape[1] // 2
    half_o = wo_in.shape[1] // 2
    depth = section_count * width
    first, last = 1, line - 2
    active = (spot >= first) & (spot <= last)
    has_guest = (spot == first) | (spot == last)
    near = jnp.where(spot * 2 < line, 1, -1)
    guest_spot = spot - near
    guest = me - 2 * near
    host = me + 2 * near

    def rows_of(block, size):
        return pl.ds(pl.multiple_of(block * size, size), size)

    def full(chunk, block):
        if chunk == KEY:
            return wk.at[rows_of(block, wk_in.shape[0]), :]
        if chunk == VALUE:
            return wv.at[rows_of(block, wv_in.shape[0]), :]
        if chunk in (QUERY_A, QUERY_B):
            return wq.at[chunk - QUERY_A, rows_of(block, wq_in.shape[0]), :]
        if chunk in (PANEL, GUEST_PANEL):
            return panel.at[rows_of(block, capacity), :]
        return wo.at[chunk - OUT_A, rows_of(block, wo_in.shape[0]), :]

    def own(chunk):
        if chunk == KEY:
            return wk_in
        if chunk == VALUE:
            return wv_in
        if chunk in (QUERY_A, QUERY_B):
            return wq_in.at[:, pl.ds((chunk - QUERY_A) * half_q, half_q)]
        return wo_in.at[:, pl.ds((chunk - OUT_A) * half_o, half_o)]

    def transfer(chunk, block, send_sem, target, mine):
        return pltpu.make_async_remote_copy(
            src_ref=own(chunk) if mine else full(chunk, block),
            dst_ref=full(chunk, block),
            send_sem=send_sem,
            recv_sem=recv.at[min(chunk, PANEL), block],
            device_id={"seq": target},
            device_id_type=MESH,
        )

    def along(chunk, source, sign, mine):
        way = (1 - sign) // 2
        return transfer(
            chunk, source * 2 + core, send_line.at[way, min(chunk, PANEL), source], me + 2 * sign, mine
        )

    def across(chunk, source, mine):
        return transfer(
            chunk, source * 2 + core, send_pair.at[min(chunk, PANEL), source], pair, mine
        )

    def onward(sign):
        return (spot + sign >= first) & (spot + sign <= last)

    def begin(chunk, source):
        mine = chunk < PANEL
        for sign in (1, -1):

            @pl.when(onward(sign))
            def _():
                along(chunk, source, sign, mine).start()

        @pl.when(active)
        def _():
            across(chunk, source, mine).start()

    def relay(chunk, step, sign):
        source = spot - sign * step
        low, high = (first, last) if chunk >= PANEL else (0, line - 1)
        valid = active & (source >= low) & (source <= high)
        if chunk == GUEST_PANEL:
            valid = active & (source == jnp.where(sign > 0, first, last))
            source = source - sign

        @pl.when(valid)
        def _():
            across(chunk, source, False).wait_recv()

            @pl.when(onward(sign))
            def _():
                along(chunk, source, sign, False).start()

            across(chunk, source, False).start()

    def relay_all(chunks, low, high, sides=(1, -1)):
        def body(step):
            for side in sides:
                for chunk in chunks:
                    relay(chunk, step, side * near)

        repeat(low, high, body)

    def await_pair(chunk):
        def body(source):
            transfer(
                chunk, source * 2 + 1 - core, send_pair.at[chunk, source], pair, False
            ).wait_recv()

        repeat(0, line, body)

    def finish_sends(chunk):
        def body(source):
            for sign in (1, -1):
                origin = jnp.clip(source, first, last) if chunk == PANEL else source

                @pl.when(onward(sign) & (origin * sign <= spot * sign))
                def _():
                    along(chunk, source, sign, False).wait_send()

            @pl.when(active)
            def _():
                across(chunk, source, False).wait_send()

        if chunk == PANEL:

            def guarded(source):
                pl.when(active)(lambda: body(source))

            repeat(0, line, guarded)
        else:
            repeat(0, line, body)

    def own_copy(chunk):
        return pltpu.make_async_copy(own(chunk), full(chunk, me), own_sem.at[chunk])

    def spread(buffer, send, receive, who, offset):
        peer = lax.rem(section + offset, section_count)
        from_input = buffer is rows_all and who == 0
        return pltpu.make_async_remote_copy(
            src_ref=picked_ref if from_input else buffer.at[section, who],
            dst_ref=buffer.at[section, who],
            send_sem=send.at[who, offset],
            recv_sem=receive.at[who, section],
            device_id={"section": peer},
            device_id_type=MESH,
        )

    def await_spread(buffer, send, receive, who):
        for offset in range(1, section_count):
            peer = lax.rem(section + offset, section_count)
            pltpu.make_async_remote_copy(
                src_ref=buffer.at[peer, who],
                dst_ref=buffer.at[peer, who],
                send_sem=send.at[who, offset],
                recv_sem=receive.at[who, peer],
                device_id={"section": peer},
                device_id_type=MESH,
            ).wait_recv()

    def to_host():
        return (
            pltpu.make_async_remote_copy(
                src_ref=picked_ref,
                dst_ref=rows_all.at[section, 1],
                send_sem=guest_send.at[0],
                recv_sem=guest_recv.at[0],
                device_id={"seq": host},
                device_id_type=MESH,
            ),
            pltpu.make_async_remote_copy(
                src_ref=gate_ref,
                dst_ref=gate_rows.at[1],
                send_sem=guest_send.at[1],
                recv_sem=guest_recv.at[1],
                device_id={"seq": host},
                device_id_type=MESH,
            ),
        )

    def give_back(half, target):
        return pltpu.make_async_remote_copy(
            src_ref=results.at[half],
            dst_ref=returned.at[half],
            send_sem=back_send.at[half],
            recv_sem=back_recv.at[half],
            device_id={"seq": target},
            device_id_type=MESH,
        )

    rows_all[section, 0] = picked_ref[...]
    gate_rows[0] = gate_ref[...]

    barrier = pltpu.get_barrier_semaphore()

    @pl.when(spot + 1 < line)
    def _():
        pl.semaphore_signal(barrier, inc=1, device_id={"seq": me + 2}, device_id_type=MESH)

    @pl.when(spot > 0)
    def _():
        pl.semaphore_signal(barrier, inc=1, device_id={"seq": me - 2}, device_id_type=MESH)

    pl.semaphore_signal(barrier, inc=1, device_id={"seq": pair}, device_id_type=MESH)
    for offset in range(1, section_count):
        peer = lax.rem(section + offset, section_count)
        pl.semaphore_signal(barrier, inc=1, device_id={"section": peer}, device_id_type=MESH)
    neighbours = jnp.where(spot + 1 < line, 1, 0) + jnp.where(spot > 0, 1, 0)
    pl.semaphore_wait(barrier, section_count + neighbours)

    weights_chunks = (KEY, VALUE, QUERY_A, QUERY_B, OUT_A, OUT_B)

    @pl.when(jnp.logical_not(active))
    def _():
        for copy in to_host():
            copy.start()
        for chunk in weights_chunks:
            begin(chunk, spot)

    def gate_column(who):
        wide = gate_rows[who]
        square = lax.broadcasted_iota(jnp.int32, (BLOCK, BLOCK), 0) == lax.broadcasted_iota(
            jnp.int32, (BLOCK, BLOCK), 1
        )
        return jnp.concatenate(
            [
                jnp.sum(jnp.where(square, wide[slot : slot + 1, :], 0.0), axis=1, keepdims=True)
                for slot in range(slots)
            ],
            axis=0,
        )

    def normalise(who):
        square_sum = jnp.zeros((capacity, 1), jnp.float32)
        for part in range(section_count):
            features = rows_all[part, who].astype(jnp.float32)
            square_sum += jnp.sum(features * features, axis=-1, keepdims=True)
        factor = lax.rsqrt(square_sum / depth + EPSILON)
        for part in range(section_count):
            cols = pl.ds(part * width, width)
            normed_ref[pl.ds(who * capacity, capacity), cols] = (
                rows_all[part, who].astype(jnp.float32) * factor * gain_ref[:, cols]
            ).astype(jnp.bfloat16)

    def attend(who, owner):
        scale = HEAD_DIM ** (-0.5)
        total = seq_count * capacity
        tile = key_slot_ref.shape[1]
        tall = lax.broadcasted_iota(jnp.int32, (ratio * capacity, 1), 0)
        query_slot = lax.rem(tall, capacity) + owner * capacity
        for group in range(groups):
            numer_ref[...] = jnp.zeros_like(numer_ref)
            denom_ref[...] = jnp.zeros_like(denom_ref)

            def fold(index):
                start = index * tile
                key_slot = key_slot_ref[pl.ds(index, 1), :]
                rows = pl.ds(pl.multiple_of(start, tile), tile)
                keys = panel[rows, pl.ds(group * HEAD_DIM, HEAD_DIM)]
                values = panel[rows, pl.ds(kv_cols + group * HEAD_DIM, HEAD_DIM)]
                wide = queries_ref[who, pl.ds(group * ratio, ratio)].reshape(
                    ratio * capacity, HEAD_DIM
                )
                scores = (
                    lax.dot_general(
                        wide, keys, (((1,), (1,)), ((), ())), preferred_element_type=jnp.float32
                    )
                    * scale
                )
                weights = jnp.where(key_slot <= query_slot, jnp.exp(scores), 0.0)
                denom_ref[...] += jnp.sum(weights, axis=-1, keepdims=True)
                numer_ref[...] += jnp.dot(
                    weights.astype(jnp.bfloat16), values, preferred_element_type=jnp.float32
                )

            repeat(0, total // tile, fold)
            safe = jnp.where(denom_ref[...] > 0, denom_ref[...], 1.0)
            result = (numer_ref[...] / safe).astype(jnp.bfloat16)
            for head in range(ratio):
                cols = pl.ds((group * ratio + head) * HEAD_DIM, HEAD_DIM)
                heads_all[section, who, :, cols] = result[head * capacity : (head + 1) * capacity]

    def finish(who, half):
        update = jnp.zeros((capacity, half_o), jnp.float32)
        head_cols = heads_all.shape[3]
        for part in range(section_count):
            update += jnp.dot(
                heads_all[part, who],
                wo[half, pl.ds(part * head_cols, head_cols), :],
                preferred_element_type=jnp.float32,
            )
        cols = pl.ds(half * half_o, half_o)
        return (
            rows_all[section, who, :, cols].astype(jnp.float32) + gate_column(who) * update
        ).astype(out_ref.dtype)

    @pl.when(active)
    def _():
        begin(KEY, spot)
        begin(VALUE, spot)
        for offset in range(1, section_count):
            spread(rows_all, rows_send, rows_recv, 0, offset).start()

        @pl.when(has_guest)
        def _():
            for copy in to_host():
                copy.wait_recv()
            for offset in range(1, section_count):
                spread(rows_all, rows_send, rows_recv, 1, offset).start()

        for chunk in weights_chunks:
            own_copy(chunk).start()
        relay_all((KEY, VALUE), 1, 2, (1,))
        begin(QUERY_A, spot)
        begin(QUERY_B, spot)
        relay_all((KEY, VALUE), 1, 2, (-1,))
        relay_all((KEY, VALUE), 2, line)
        await_spread(rows_all, rows_send, rows_recv, 0)
        normalise(0)
        relay_all((QUERY_A, QUERY_B), 1, 2, (1,))

        @pl.when(has_guest)
        def _():
            await_spread(rows_all, rows_send, rows_recv, 1)
            normalise(1)

        for chunk in (KEY, VALUE):
            await_pair(chunk)
            own_copy(chunk).wait()
        for position, weight in enumerate((wk, wv)):
            sums = jnp.dot(
                normed_ref[...], weight[...], preferred_element_type=jnp.float32
            ).astype(jnp.bfloat16)
            cols = pl.ds(position * kv_cols, kv_cols)
            panel[rows_of(me, capacity), cols] = sums[:capacity]

            @pl.when(has_guest)
            def _():
                panel[rows_of(guest, capacity), cols] = sums[capacity:]

        begin(PANEL, spot)

        @pl.when(has_guest)
        def _():
            begin(GUEST_PANEL, guest_spot)

        begin(OUT_A, spot)
        begin(OUT_B, spot)
        relay_all((QUERY_A, QUERY_B), 1, 2, (-1,))
        relay_all((QUERY_A, QUERY_B), 2, line)
        relay_all((PANEL, GUEST_PANEL), 1, line)
        relay_all((OUT_A, OUT_B), 1, 2, (1,))
        heads_half = half_q // HEAD_DIM
        for half in range(2):
            await_pair(QUERY_A + half)
            own_copy(QUERY_A + half).wait()
            sums = jnp.dot(
                normed_ref[...], wq[half], preferred_element_type=jnp.float32
            ).astype(jnp.bfloat16)
            for who in range(2):
                for head in range(heads_half):
                    queries_ref[who, half * heads_half + head] = sums[
                        who * capacity : (who + 1) * capacity,
                        head * HEAD_DIM : (head + 1) * HEAD_DIM,
                    ]
        await_pair(PANEL)

        @pl.when(has_guest)
        def _():
            attend(1, guest)
            for offset in range(1, section_count):
                spread(heads_all, heads_send, heads_recv, 1, offset).start()

        attend(0, me)
        for offset in range(1, section_count):
            spread(heads_all, heads_send, heads_recv, 0, offset).start()
        relay_all((OUT_A, OUT_B), 1, 2, (-1,))
        relay_all((OUT_A, OUT_B), 2, line)
        for half in range(2):
            await_pair(OUT_A + half)
            own_copy(OUT_A + half).wait()

        @pl.when(has_guest)
        def _():
            await_spread(heads_all, heads_send, heads_recv, 1)
            for half in range(2):
                results[half] = finish(1, half)
                give_back(half, guest).start()

        await_spread(heads_all, heads_send, heads_recv, 0)
        for half in range(2):
            out_ref[:, pl.ds(half * half_o, half_o)] = finish(0, half)
        for offset in range(1, section_count):
            spread(rows_all, rows_send, rows_recv, 0, offset).wait_send()
            spread(heads_all, heads_send, heads_recv, 0, offset).wait_send()

        @pl.when(has_guest)
        def _():
            for offset in range(1, section_count):
                spread(rows_all, rows_send, rows_recv, 1, offset).wait_send()
                spread(heads_all, heads_send, heads_recv, 1, offset).wait_send()
            for half in range(2):
                give_back(half, guest).wait_send()

    for chunk in weights_chunks + (PANEL,):
        finish_sends(chunk)

    @pl.when(jnp.logical_not(active))
    def _():
        for copy in to_host():
            copy.wait_send()
        for half in range(2):
            give_back(half, host).wait_recv()
            out_ref[:, pl.ds(half * half_o, half_o)] = returned[half]


def pick(
    seq_count, tokens_ref, gate_ref, chosen_ref, count_ref, picked_ref, gates_ref, key_slot_ref, sems
):
    me = lax.axis_index("seq")
    slots = chosen_ref.shape[1]
    tiles, tile = key_slot_ref.shape
    total = tiles * tile

    def rows_copy(slot):
        start = pl.multiple_of(chosen_ref[me, slot] * BLOCK, BLOCK)
        return pltpu.make_async_copy(
            tokens_ref.at[pl.ds(start, BLOCK), :],
            picked_ref.at[pl.ds(slot * BLOCK, BLOCK), :],
            sems.at[slot],
        )

    for slot in range(slots):
        rows_copy(slot).start()
    lane = lax.broadcasted_iota(jnp.int32, (1, tile), 1)

    def fill(index):
        key_slot = lane + index * tile
        for piece in range(tile // BLOCK):
            number = index * (tile // BLOCK) + piece
            live = lax.rem(number, slots) < count_ref[number // slots]
            beyond = jnp.where(live, 0, total)
            key_slot = key_slot + jnp.where(lane // BLOCK == piece, beyond, 0)
        key_slot_ref[pl.ds(index, 1), :] = key_slot

    repeat(0, tiles, fill)
    for slot in range(slots):
        gates_ref[pl.ds(slot, 1), :] = gate_ref[pl.ds(chosen_ref[me, slot], 1), :]
    for slot in range(slots):
        rows_copy(slot).wait()


def local(
    tokens, norm_gain, w_query, w_key, w_value, w_out, router_gate, chosen_blocks, block_counts
):
    seq_count = lax.axis_size("seq")
    section_count = lax.axis_size("section")
    me = lax.axis_index("seq")
    tok_rows, width = tokens.shape
    slots = chosen_blocks.shape[1]
    capacity = slots * BLOCK
    depth = section_count * width
    query_cols = w_query.shape[1]
    kv_cols = w_key.shape[1]
    ratio = HEADS // KV_HEADS
    line = seq_count // 2

    vmem = pl.BlockSpec(memory_space=pltpu.VMEM)
    smem = pl.BlockSpec(memory_space=pltpu.SMEM)
    anywhere = pl.BlockSpec(memory_space=pl.ANY)
    bf16 = jnp.bfloat16
    dma = pltpu.SemaphoreType.DMA
    tile = math.gcd(seq_count * capacity, 512)
    picked, gates, key_slot = pl.pallas_call(
        functools.partial(pick, seq_count),
        out_shape=(
            jax.ShapeDtypeStruct((capacity, width), tokens.dtype),
            jax.ShapeDtypeStruct((slots, BLOCK), jnp.float32),
            jax.ShapeDtypeStruct((seq_count * capacity // tile, tile), jnp.int32),
        ),
        in_specs=[anywhere, vmem, smem, smem],
        out_specs=(vmem, vmem, vmem),
        scratch_shapes=[dma((slots,))],
    )(tokens, router_gate.reshape(tok_rows // BLOCK, BLOCK), chosen_blocks, block_counts)
    new_rows = pl.pallas_call(
        functools.partial(kernel, seq_count, section_count),
        out_shape=jax.ShapeDtypeStruct((capacity, width), tokens.dtype),
        in_specs=[vmem] * 4 + [anywhere] * 4,
        out_specs=vmem,
        scratch_shapes=[
            pltpu.VMEM((section_count, 2, capacity, width), bf16),
            pltpu.VMEM((2, slots, BLOCK), jnp.float32),
            pltpu.VMEM((2 * capacity, depth), bf16),
            pltpu.VMEM((depth, kv_cols), bf16),
            pltpu.VMEM((depth, kv_cols), bf16),
            pltpu.VMEM((2, depth, query_cols // 2), bf16),
            pltpu.VMEM((2, w_out.shape[0] * seq_count, w_out.shape[1] // 2), bf16),
            pltpu.VMEM((seq_count * capacity, 2 * kv_cols), bf16),
            pltpu.VMEM((2, query_cols // HEAD_DIM, capacity, HEAD_DIM), bf16),
            pltpu.VMEM((ratio * capacity, HEAD_DIM), jnp.float32),
            pltpu.VMEM((ratio * capacity, 1), jnp.float32),
            pltpu.VMEM((section_count, 2, capacity, query_cols), bf16),
            pltpu.VMEM((2, capacity, width // 2), bf16),
            pltpu.VMEM((2, capacity, width // 2), bf16),
            dma((7, seq_count)),
            dma((2, 7, line)),
            dma((7, line)),
            dma((6,)),
            dma((2, section_count)),
            dma((2, section_count)),
            dma((2, section_count)),
            dma((2, section_count)),
            dma((2,)),
            dma((2,)),
            dma((2,)),
            dma((2,)),
        ],
        compiler_params=pltpu.CompilerParams(collective_id=0, has_side_effects=True),
    )(
        picked,
        norm_gain[None, :],
        gates,
        key_slot,
        w_query,
        w_key,
        w_value,
        w_out,
    )
    mixed = tokens.reshape(tok_rows // BLOCK, BLOCK, width)
    number = lax.broadcasted_iota(jnp.int32, (tok_rows // BLOCK, 1, 1), 0)
    for slot in range(slots):
        hit = (number == chosen_blocks[me, slot]) & (slot < block_counts[me])
        mixed = jnp.where(hit, new_rows[None, slot * BLOCK : (slot + 1) * BLOCK], mixed)
    return mixed.reshape(tok_rows, width)


def solution(mesh):
    return jax.shard_map(
        local,
        mesh=mesh,
        in_specs=(
            P("seq", "section"),
            P(),
            P("seq", "section"),
            P("seq", "section"),
            P("seq", "section"),
            P("seq", "section"),
            P("seq"),
            P(),
            P(),
        ),
        out_specs=P("seq", "section"),
        check_vma=False,
    )
```

time: 69.9 us -> 59.8 us (0.86)
  Pallas kernels: 57.6 us -> 53.1 us
  between operations: 3.14 us -> 0.7 us
  other arithmetic: 4.2 us -> 2.49 us
  local copies, waits for them, and re-layouts: 4.43 us -> 3.22 us
    pallas_call x1, Pallas kernels: 57.6 us -> 50.7 us  [local(): pl.pallas_call(functools.partial(kernel, seq_count, section_count), out_s...]
    pallas_call x0 -> x1, Pallas kernels: none -> 2.45 us  [local(): pl.pallas_call(functools.partial(pick, seq_count), out_shape=(jax.ShapeDt...]
    select_n x1, other arithmetic: 0.07 us -> 1.84 us  [local(): jnp.where(hit, new_rows[None, slot * BLOCK:(slot + 1) * BLOCK], mixed)]
    dynamic_update_slice x1 -> x0, other arithmetic: 1.66 us -> none  [local(): mixed = lax.dynamic_update_slice_in_dim(mixed, chosen, start, 0)]
    convert_element_type x1 -> x0, other arithmetic: 1.24 us -> none  [local(): (jnp.arange(capacity, dtype=jnp.int32) // BLOCK < my_count).astype(jnp.in...]
    broadcast_in_dim x2 -> x1, local copies, waits for them, and re-layouts: 0.82 us -> 0.07 us  [local(): jnp.where(hit, new_rows[None, slot * BLOCK:(slot + 1) * BLOCK], mixed)]
    unnamed x9 -> x7, local copies, waits for them, and re-layouts: 1.74 us -> 1.98 us
where the time goes in v2:
time: 59.8 us; the launch traced here: 59.5 us
  Pallas kernels  53.1 us (89%)
  local copies, waits for them, and re-layouts  3.22 us (5%)
  other arithmetic  2.49 us (4%)
  between operations  0.7 us (1%)
    pallas_call x1, Pallas kernels, local(): pl.pallas_call(functools.partial(kernel, seq_count, section_count), out_s...  50.7 us
    pallas_call x1, Pallas kernels, local(): pl.pallas_call(functools.partial(pick, seq_count), out_shape=(jax.ShapeDt...  2.45 us
    unnamed x7, local copies, waits for them, and re-layouts  1.98 us
    select_n x1, other arithmetic, local(): jnp.where(hit, new_rows[None, slot * BLOCK:(slot + 1) * BLOCK], mixed)  1.84 us

profile of v2, /device:TPU:0, one launch (start us, length us, event | category | flops | bytes accessed | tf_op | source)
XLA Modules:
  0.0 59.5 jit_solution(15234275284159931113)
XLA Ops:
  0.0 0.0 copy-start.1
  0.0 0.7 %copy-done.1 = s32[8]{0:T(128)S(1)} copy-done((s32[8]{0:T(128)S(1)}, s32[8]{0:T(128)}, u32[]{:S(2)}) %copy-start.1) | copy-done | bytes 56
  0.7 0.6 dynamic_slice.7
  1.9 0.0 copy-start.2
  1.9 0.6 %copy-done.2 = s32[8,1]{0,1:T(1,128)S(1)} copy-done((s32[8,1]{0,1:T(1,128)S(1)}, s32[8,1]{0,1:T(1,128)}, u32[]{:S(2)}) %copy-start.2) | copy-done | bytes 56
  2.6 0.6 constant_dynamic-slice_fusion
  3.1 0.7 %compare_and_fusion = pred[4]{0:T(512)(128)(4,1)S(1)} fusion(pred[]{:T(512)} %bitcast.1, s32[]{:T(128)} %bitcast), kind=kLoop, calls=%fused_computation.1 | loop fusion | flops 8 | bytes 9 | tf_op jit(solution)/shard_map/and | solution.py:608
  3.8 0.1 broadcast_bitcast_fusion
  3.9 0.7 %copy.10.chosen_ref = s32[8,1]{1,0:T(8,128)} copy(s32[8,1]{0,1:T(1,128)S(1)} %copy-done.2) | data formatting | bytes 64 | tf_op args[7]
  4.5 2.4 %shard_map.91 = (bf16[128,512]{1,0:T(8,128)(2,1)}, f32[1,128]{1,0:T(1,128)}, s32[2,512]{1,0:T(2,128)}) custom-call(bf16[512,512]{1,0:T(8,128)(2,1)} %tokens_ref.1, f32[4,128]{1,0:T(4,128)} %bitcast.9, s32[8,1]{1,0:T(8,128)} %copy.10.chosen_ref, s32[8]{0:T(128)} %count_ref.1), custom_call_target="tpu_custom_call" | custom-call | tf_op jit(solution)/shard_map/pallas_call | solution.py:550
  7.0 0.0 copy-start
  7.0 50.7 %shard_map.92 = bf16[128,512]{1,0:T(8,128)(2,1)} custom-call(bf16[128,512]{1,0:T(8,128)(2,1)} %get-tuple-element.8.picked_ref, f32[1,2048]{1,0:T(1,128)} %bitcast.8, f32[1,128]{1,0:T(1,128)} %get-tuple-element.9.gate_ref, s32[2,512]{1,0:T(2,128)} %get-tuple-element.10.key_slot_ref, bf16[256,512]{1,0:T(8,128)(2,1)} %wq_in.1, bf16[256,128]{1,0:T(8,128)(2,1)} %wk_in.1, ...), custom_call_target="tpu_custom_call" | custom-call | tf_op jit(solution)/shard_map/pallas_call | solution.py:561
  57.7 0.0 copy-done
  57.7 1.8 %bitcast_select_fusion = bf16[512,512]{1,0:T(8,128)(2,1)} fusion(bf16[512,512]{1,0:T(8,128)(2,1)S(1)} %copy-done, pred[512]{0:T(512)(128)(4,1)S(1)} %broadcast_bitcast_fusion, bf16[128,512]{1,0:T(8,128)(2,1)} %shard_map.92), kind=kLoop, calls=%fused_computation | loop fusion | flops 262144 | bytes 1180160 | tf_op jit(solution)/shard_map/jit(_where)/select_n | solution.py:609
Async XLA Ops:
  0.0 0.7 %copy-start.1 = (s32[8]{0:T(128)S(1)}, s32[8]{0:T(128)}, u32[]{:S(2)}) copy-start(s32[8]{0:T(128)} %count_ref.1) | copy-start | bytes 100
  1.9 0.7 %copy-start.2 = (s32[8,1]{0,1:T(1,128)S(1)}, s32[8,1]{0,1:T(1,128)}, u32[]{:S(2)}) copy-start(s32[8,1]{0,1:T(1,128)} %param.16) | copy-start | bytes 100
  7.0 50.7 %copy-start = (bf16[512,512]{1,0:T(8,128)(2,1)S(1)}, bf16[512,512]{1,0:T(8,128)(2,1)}, u32[]{:S(2)}) copy-start(bf16[512,512]{1,0:T(8,128)(2,1)} %tokens_ref.1) | copy-start | bytes 1572868

commit v3 on v2

--- a/solution.py
+++ b/solution.py
@@ -34,10 +34,11 @@
 def kernel(
     seq_count,
     section_count,
-    picked_ref,
+    tokens_ref,
     gain_ref,
     gate_ref,
-    key_slot_ref,
+    chosen_ref,
+    count_ref,
     wq_in,
     wk_in,
     wv_in,
@@ -69,6 +70,7 @@
     guest_recv,
     back_send,
     back_recv,
+    key_slots,
 ):
     me = lax.axis_index("seq")
     section = lax.axis_index("section")
@@ -76,7 +78,7 @@
     spot = me // 2
     core = lax.rem(me, 2)
     pair = spot * 2 + 1 - core
-    slots = gate_ref.shape[0]
+    slots = chosen_ref.shape[0] // seq_count
     capacity, width = out_ref.shape
     kv_cols = wk_in.shape[1]
     groups = kv_cols // HEAD_DIM
@@ -212,9 +214,8 @@
 
     def spread(buffer, send, receive, who, offset):
         peer = lax.rem(section + offset, section_count)
-        from_input = buffer is rows_all and who == 0
         return pltpu.make_async_remote_copy(
-            src_ref=picked_ref if from_input else buffer.at[section, who],
+            src_ref=buffer.at[section, who],
             dst_ref=buffer.at[section, who],
             send_sem=send.at[who, offset],
             recv_sem=receive.at[who, section],
@@ -237,7 +238,7 @@
     def to_host():
         return (
             pltpu.make_async_remote_copy(
-                src_ref=picked_ref,
+                src_ref=rows_all.at[section, 0],
                 dst_ref=rows_all.at[section, 1],
                 send_sem=guest_send.at[0],
                 recv_sem=guest_recv.at[0],
@@ -245,7 +246,7 @@
                 device_id_type=MESH,
             ),
             pltpu.make_async_remote_copy(
-                src_ref=gate_ref,
+                src_ref=gate_rows.at[0],
                 dst_ref=gate_rows.at[1],
                 send_sem=guest_send.at[1],
                 recv_sem=guest_recv.at[1],
@@ -264,8 +265,39 @@
             device_id_type=MESH,
         )
 
-    rows_all[section, 0] = picked_ref[...]
-    gate_rows[0] = gate_ref[...]
+    for slot in range(slots):
+        number = chosen_ref[me * slots + slot]
+        rows = tokens_ref[:BLOCK, :]
+        gates = gate_ref[:1, :]
+        for block in range(1, gate_ref.shape[0]):
+            rows = jnp.where(
+                jnp.full(rows.shape, number, jnp.int32) == block,
+                tokens_ref[block * BLOCK : (block + 1) * BLOCK, :],
+                rows,
+            )
+            gates = jnp.where(
+                jnp.full(gates.shape, number, jnp.int32) == block,
+                gate_ref[block : block + 1, :],
+                gates,
+            )
+        rows_all[section, 0, pl.ds(slot * BLOCK, BLOCK), :] = rows
+        gate_rows[0, pl.ds(slot, 1), :] = gates
+    total = seq_count * capacity
+    tiles, tile = key_slots.shape
+    lane = lax.broadcasted_iota(jnp.int32, (1, tile), 1)
+
+    def fill(index):
+        key_slot = lane + index * tile
+        for piece in range(tile // BLOCK):
+            place = index * (tile // BLOCK) + piece
+            within = lax.rem(place, slots)
+            count = jnp.full((1, tile), count_ref[place // slots], jnp.int32)
+            key_slot = jnp.where(
+                (lane // BLOCK == piece) & (count <= within), total, key_slot
+            )
+        key_slots[pl.ds(index, 1), :] = key_slot
+
+    repeat(0, tiles, fill)
 
     barrier = pltpu.get_barrier_semaphore()
 
@@ -320,8 +352,6 @@
 
     def attend(who, owner):
         scale = HEAD_DIM ** (-0.5)
-        total = seq_count * capacity
-        tile = key_slot_ref.shape[1]
         tall = lax.broadcasted_iota(jnp.int32, (ratio * capacity, 1), 0)
         query_slot = lax.rem(tall, capacity) + owner * capacity
         for group in range(groups):
@@ -330,7 +360,7 @@
 
             def fold(index):
                 start = index * tile
-                key_slot = key_slot_ref[pl.ds(index, 1), :]
+                key_slot = key_slots[pl.ds(index, 1), :]
                 rows = pl.ds(pl.multiple_of(start, tile), tile)
                 keys = panel[rows, pl.ds(group * HEAD_DIM, HEAD_DIM)]
                 values = panel[rows, pl.ds(kv_cols + group * HEAD_DIM, HEAD_DIM)]
@@ -490,40 +520,16 @@
             out_ref[:, pl.ds(half * half_o, half_o)] = returned[half]
 
 
-def pick(
-    seq_count, tokens_ref, gate_ref, chosen_ref, count_ref, picked_ref, gates_ref, key_slot_ref, sems
-):
+def put(tokens_ref, rows_ref, chosen_ref, count_ref, mixed_ref):
     me = lax.axis_index("seq")
-    slots = chosen_ref.shape[1]
-    tiles, tile = key_slot_ref.shape
-    total = tiles * tile
-
-    def rows_copy(slot):
-        start = pl.multiple_of(chosen_ref[me, slot] * BLOCK, BLOCK)
-        return pltpu.make_async_copy(
-            tokens_ref.at[pl.ds(start, BLOCK), :],
-            picked_ref.at[pl.ds(slot * BLOCK, BLOCK), :],
-            sems.at[slot],
-        )
-
+    mixed_ref[...] = tokens_ref[...]
+    slots = rows_ref.shape[0] // BLOCK
     for slot in range(slots):
-        rows_copy(slot).start()
-    lane = lax.broadcasted_iota(jnp.int32, (1, tile), 1)
-
-    def fill(index):
-        key_slot = lane + index * tile
-        for piece in range(tile // BLOCK):
-            number = index * (tile // BLOCK) + piece
-            live = lax.rem(number, slots) < count_ref[number // slots]
-            beyond = jnp.where(live, 0, total)
-            key_slot = key_slot + jnp.where(lane // BLOCK == piece, beyond, 0)
-        key_slot_ref[pl.ds(index, 1), :] = key_slot
-
-    repeat(0, tiles, fill)
-    for slot in range(slots):
-        gates_ref[pl.ds(slot, 1), :] = gate_ref[pl.ds(chosen_ref[me, slot], 1), :]
-    for slot in range(slots):
-        rows_copy(slot).wait()
+
+        @pl.when(slot < count_ref[me])
+        def _():
+            start = pl.multiple_of(chosen_ref[me * slots + slot] * BLOCK, BLOCK)
+            mixed_ref[pl.ds(start, BLOCK), :] = rows_ref[slot * BLOCK : (slot + 1) * BLOCK, :]
 
 
 def local(
@@ -531,7 +537,6 @@
 ):
     seq_count = lax.axis_size("seq")
     section_count = lax.axis_size("section")
-    me = lax.axis_index("seq")
     tok_rows, width = tokens.shape
     slots = chosen_blocks.shape[1]
     capacity = slots * BLOCK
@@ -547,21 +552,11 @@
     bf16 = jnp.bfloat16
     dma = pltpu.SemaphoreType.DMA
     tile = math.gcd(seq_count * capacity, 512)
-    picked, gates, key_slot = pl.pallas_call(
-        functools.partial(pick, seq_count),
-        out_shape=(
-            jax.ShapeDtypeStruct((capacity, width), tokens.dtype),
-            jax.ShapeDtypeStruct((slots, BLOCK), jnp.float32),
-            jax.ShapeDtypeStruct((seq_count * capacity // tile, tile), jnp.int32),
-        ),
-        in_specs=[anywhere, vmem, smem, smem],
-        out_specs=(vmem, vmem, vmem),
-        scratch_shapes=[dma((slots,))],
-    )(tokens, router_gate.reshape(tok_rows // BLOCK, BLOCK), chosen_blocks, block_counts)
+    blocks = chosen_blocks.reshape(-1)
     new_rows = pl.pallas_call(
         functools.partial(kernel, seq_count, section_count),
         out_shape=jax.ShapeDtypeStruct((capacity, width), tokens.dtype),
-        in_specs=[vmem] * 4 + [anywhere] * 4,
+        in_specs=[vmem] * 3 + [smem] * 2 + [anywhere] * 4,
         out_specs=vmem,
         scratch_shapes=[
             pltpu.VMEM((section_count, 2, capacity, width), bf16),
@@ -590,24 +585,26 @@
             dma((2,)),
             dma((2,)),
             dma((2,)),
+            pltpu.VMEM((seq_count * capacity // tile, tile), jnp.int32),
         ],
         compiler_params=pltpu.CompilerParams(collective_id=0, has_side_effects=True),
     )(
-        picked,
+        tokens,
         norm_gain[None, :],
-        gates,
-        key_slot,
+        router_gate.reshape(tok_rows // BLOCK, BLOCK),
+        blocks,
+        block_counts,
         w_query,
         w_key,
         w_value,
         w_out,
     )
-    mixed = tokens.reshape(tok_rows // BLOCK, BLOCK, width)
-    number = lax.broadcasted_iota(jnp.int32, (tok_rows // BLOCK, 1, 1), 0)
-    for slot in range(slots):
-        hit = (number == chosen_blocks[me, slot]) & (slot < block_counts[me])
-        mixed = jnp.where(hit, new_rows[None, slot * BLOCK : (slot + 1) * BLOCK], mixed)
-    return mixed.reshape(tok_rows, width)
+    return pl.pallas_call(
+        put,
+        out_shape=jax.ShapeDtypeStruct(tokens.shape, tokens.dtype),
+        in_specs=[vmem, vmem, smem, smem],
+        out_specs=vmem,
+    )(tokens, new_rows, blocks, block_counts)
 
 
 def solution(mesh):

time: 59.8 us -> 52.8 us (0.88)
  local copies, waits for them, and re-layouts: 3.22 us -> 0 us
  other arithmetic: 2.49 us -> 0 us
  between operations: 0.7 us -> 0.01 us
    unnamed x7 -> x0, local copies, waits for them, and re-layouts: 1.98 us -> none
    select_n x1 -> x0, other arithmetic: 1.84 us -> none  [local(): jnp.where(hit, new_rows[None, slot * BLOCK:(slot + 1) * BLOCK], mixed)]
    dynamic_slice x2 -> x0, local copies, waits for them, and re-layouts: 1.16 us -> none  [local(): hit = (number == chosen_blocks[me, slot]) & (slot < block_counts[me])]
    and x1 -> x0, other arithmetic: 0.65 us -> none  [local(): hit = (number == chosen_blocks[me, slot]) & (slot < block_counts[me])]
where the time goes in v3:
time: 52.8 us; the launch traced here: 52.7 us
  Pallas kernels  52.7 us (100%)
    pallas_call x1, Pallas kernels, local(): pl.pallas_call(functools.partial(kernel, seq_count, section_count), out_s...  50.8 us
    pallas_call x1, Pallas kernels, local(): pl.pallas_call(put, out_shape=jax.ShapeDtypeStruct(tokens.shape, tokens.d...  1.92 us

profile of v3, /device:TPU:0, one launch (start us, length us, event | category | flops | bytes accessed | tf_op | source)
XLA Modules:
  0.0 52.7 jit_solution(2832289744355667759)
XLA Ops:
  0.0 50.8 %shard_map.91.rows_ref = bf16[128,512]{1,0:T(8,128)(2,1)} custom-call(bf16[512,512]{1,0:T(8,128)(2,1)} %tokens_ref.3, f32[1,2048]{1,0:T(1,128)} %bitcast.3, f32[4,128]{1,0:T(4,128)} %bitcast.4, s32[8]{0:T(128)} %bitcast.5, s32[8]{0:T(128)} %count_ref.3, bf16[256,512]{1,0:T(8,128)(2,1)} %wq_in.1, bf16[256,128]{1,0:T(8,128)(2,1)} %wk_in.1, ...), custom_call_target="tpu_custom_call" | custom-call | tf_op jit(solution)/shard_map/pallas_call | solution.py:556
  50.8 1.9 %shard_map.92 = bf16[512,512]{1,0:T(8,128)(2,1)} custom-call(bf16[512,512]{1,0:T(8,128)(2,1)} %tokens_ref.3, bf16[128,512]{1,0:T(8,128)(2,1)} %shard_map.91.rows_ref, s32[8]{0:T(128)} %bitcast.6, s32[8]{0:T(128)} %count_ref.3), custom_call_target="tpu_custom_call" | custom-call | tf_op jit(solution)/shard_map/pallas_call | solution.py:602

commit v4 on v3

--- a/solution.py
+++ b/solution.py
@@ -94,6 +94,9 @@
     guest = me - 2 * near
     host = me + 2 * near
 
+    square = section_count == 4
+    offsets = (1, 2) if square else tuple(range(1, section_count))
+
     def rows_of(block, size):
         return pl.ds(pl.multiple_of(block * size, size), size)
 
@@ -212,28 +215,74 @@
     def own_copy(chunk):
         return pltpu.make_async_copy(own(chunk), full(chunk, me), own_sem.at[chunk])
 
+    def beside(offset):
+        if not square:
+            return lax.rem(section + offset, section_count)
+        if offset == 1:
+            return section + 1 - 2 * lax.rem(section, 2)
+        return section + 2 - 4 * (section // 2)
+
     def spread(buffer, send, receive, who, offset):
-        peer = lax.rem(section + offset, section_count)
         return pltpu.make_async_remote_copy(
             src_ref=buffer.at[section, who],
             dst_ref=buffer.at[section, who],
             send_sem=send.at[who, offset],
             recv_sem=receive.at[who, section],
+            device_id={"section": beside(offset)},
+            device_id_type=MESH,
+        )
+
+    def await_direct(buffer, send, receive, who, offset):
+        peer = beside(offset)
+        pltpu.make_async_remote_copy(
+            src_ref=buffer.at[peer, who],
+            dst_ref=buffer.at[peer, who],
+            send_sem=send.at[who, offset],
+            recv_sem=receive.at[who, peer],
             device_id={"section": peer},
             device_id_type=MESH,
-        )
+        ).wait_recv()
+
+    def passed_on(buffer, send, receive, who, half, block, target, mark):
+        part = buffer.at[block, who, pl.ds(half * (capacity // 2), capacity // 2), :]
+        return pltpu.make_async_remote_copy(
+            src_ref=part,
+            dst_ref=part,
+            send_sem=send.at[who, 3 * half],
+            recv_sem=receive.at[who, mark],
+            device_id={"section": target},
+            device_id_type=MESH,
+        )
+
+    def outgoing(buffer, send, receive, who, half):
+        block, target = beside(1 + half), beside(2 - half)
+        mark = target if half else block
+        return passed_on(buffer, send, receive, who, half, block, target, mark)
+
+    def pass_on(buffer, send, receive, who):
+        if square:
+            for half in range(2):
+                await_direct(buffer, send, receive, who, 1 + half)
+                outgoing(buffer, send, receive, who, half).start()
 
     def await_spread(buffer, send, receive, who):
-        for offset in range(1, section_count):
-            peer = lax.rem(section + offset, section_count)
-            pltpu.make_async_remote_copy(
-                src_ref=buffer.at[peer, who],
-                dst_ref=buffer.at[peer, who],
-                send_sem=send.at[who, offset],
-                recv_sem=receive.at[who, peer],
-                device_id={"section": peer},
-                device_id_type=MESH,
-            ).wait_recv()
+        if square:
+            block = 3 - section
+            for half in range(2):
+                mark = section if half else block
+                passed_on(
+                    buffer, send, receive, who, half, block, beside(1), mark
+                ).wait_recv()
+        else:
+            for offset in offsets:
+                await_direct(buffer, send, receive, who, offset)
+
+    def finish_spread(buffer, send, receive, who):
+        for offset in offsets:
+            spread(buffer, send, receive, who, offset).wait_send()
+        if square:
+            for half in range(2):
+                outgoing(buffer, send, receive, who, half).wait_send()
 
     def to_host():
         return (
@@ -404,14 +453,14 @@
     def _():
         begin(KEY, spot)
         begin(VALUE, spot)
-        for offset in range(1, section_count):
+        for offset in offsets:
             spread(rows_all, rows_send, rows_recv, 0, offset).start()
 
         @pl.when(has_guest)
         def _():
             for copy in to_host():
                 copy.wait_recv()
-            for offset in range(1, section_count):
+            for offset in offsets:
                 spread(rows_all, rows_send, rows_recv, 1, offset).start()
 
         for chunk in weights_chunks:
@@ -419,7 +468,13 @@
         relay_all((KEY, VALUE), 1, 2, (1,))
         begin(QUERY_A, spot)
         begin(QUERY_B, spot)
+        pass_on(rows_all, rows_send, rows_recv, 0)
         relay_all((KEY, VALUE), 1, 2, (-1,))
+
+        @pl.when(has_guest)
+        def _():
+            pass_on(rows_all, rows_send, rows_recv, 1)
+
         relay_all((KEY, VALUE), 2, line)
         await_spread(rows_all, rows_send, rows_recv, 0)
         normalise(0)
@@ -474,12 +529,18 @@
         @pl.when(has_guest)
         def _():
             attend(1, guest)
-            for offset in range(1, section_count):
+            for offset in offsets:
                 spread(heads_all, heads_send, heads_recv, 1, offset).start()
 
         attend(0, me)
-        for offset in range(1, section_count):
+        for offset in offsets:
             spread(heads_all, heads_send, heads_recv, 0, offset).start()
+
+        @pl.when(has_guest)
+        def _():
+            pass_on(heads_all, heads_send, heads_recv, 1)
+
+        pass_on(heads_all, heads_send, heads_recv, 0)
         relay_all((OUT_A, OUT_B), 1, 2, (-1,))
         relay_all((OUT_A, OUT_B), 2, line)
         for half in range(2):
@@ -496,15 +557,13 @@
         await_spread(heads_all, heads_send, heads_recv, 0)
         for half in range(2):
             out_ref[:, pl.ds(half * half_o, half_o)] = finish(0, half)
-        for offset in range(1, section_count):
-            spread(rows_all, rows_send, rows_recv, 0, offset).wait_send()
-            spread(heads_all, heads_send, heads_recv, 0, offset).wait_send()
-
-        @pl.when(has_guest)
-        def _():
-            for offset in range(1, section_count):
-                spread(rows_all, rows_send, rows_recv, 1, offset).wait_send()
-                spread(heads_all, heads_send, heads_recv, 1, offset).wait_send()
+        finish_spread(rows_all, rows_send, rows_recv, 0)
+        finish_spread(heads_all, heads_send, heads_recv, 0)
+
+        @pl.when(has_guest)
+        def _():
+            finish_spread(rows_all, rows_send, rows_recv, 1)
+            finish_spread(heads_all, heads_send, heads_recv, 1)
             for half in range(2):
                 give_back(half, guest).wait_send()
 

time: 52.8 us -> 54.5 us (1.032)
  Pallas kernels: 52.7 us -> 54.4 us
    pallas_call x1, Pallas kernels: 50.8 us -> 52.5 us  [local(): pl.pallas_call(functools.partial(kernel, seq_count, section_count), out_s...]
where the time goes in v4:
time: 54.5 us; the launch traced here: 54.4 us
  Pallas kernels  54.4 us (100%)
    pallas_call x1, Pallas kernels, local(): pl.pallas_call(functools.partial(kernel, seq_count, section_count), out_s...  52.5 us
    pallas_call x1, Pallas kernels, local(): pl.pallas_call(put, out_shape=jax.ShapeDtypeStruct(tokens.shape, tokens.d...  1.91 us

profile of v4, /device:TPU:0, one launch (start us, length us, event | category | flops | bytes accessed | tf_op | source)
XLA Modules:
  0.0 54.4 jit_solution(7583220825972266665)
XLA Ops:
  0.0 52.5 %shard_map.91.rows_ref = bf16[128,512]{1,0:T(8,128)(2,1)} custom-call(bf16[512,512]{1,0:T(8,128)(2,1)} %tokens_ref.3, f32[1,2048]{1,0:T(1,128)} %bitcast.3, f32[4,128]{1,0:T(4,128)} %bitcast.4, s32[8]{0:T(128)} %bitcast.5, s32[8]{0:T(128)} %count_ref.3, bf16[256,512]{1,0:T(8,128)(2,1)} %wq_in.1, bf16[256,128]{1,0:T(8,128)(2,1)} %wk_in.1, ...), custom_call_target="tpu_custom_call" | custom-call | tf_op jit(solution)/shard_map/pallas_call | solution.py:615
  52.5 1.9 %shard_map.92 = bf16[512,512]{1,0:T(8,128)(2,1)} custom-call(bf16[512,512]{1,0:T(8,128)(2,1)} %tokens_ref.3, bf16[128,512]{1,0:T(8,128)(2,1)} %shard_map.91.rows_ref, s32[8]{0:T(128)} %bitcast.6, s32[8]{0:T(128)} %count_ref.3), custom_call_target="tpu_custom_call" | custom-call | tf_op jit(solution)/shard_map/pallas_call | solution.py:661

commit v5 on v3

--- a/solution.py
+++ b/solution.py
@@ -480,16 +480,16 @@
         attend(0, me)
         for offset in range(1, section_count):
             spread(heads_all, heads_send, heads_recv, 0, offset).start()
-        relay_all((OUT_A, OUT_B), 1, 2, (-1,))
-        relay_all((OUT_A, OUT_B), 2, line)
         for half in range(2):
+            relay_all((OUT_A + half,), 1, 2, (-1,))
+            relay_all((OUT_A + half,), 2, line)
             await_pair(OUT_A + half)
             own_copy(OUT_A + half).wait()
 
-        @pl.when(has_guest)
-        def _():
-            await_spread(heads_all, heads_send, heads_recv, 1)
-            for half in range(2):
+            @pl.when(has_guest)
+            def _():
+                if half == 0:
+                    await_spread(heads_all, heads_send, heads_recv, 1)
                 results[half] = finish(1, half)
                 give_back(half, guest).start()
 

time: 52.8 us -> 53.1 us (level)
  no operation moved by 1% of the time
where the time goes in v5:
time: 53.1 us; the launch traced here: 52.9 us
  Pallas kernels  52.9 us (100%)
    pallas_call x1, Pallas kernels, local(): pl.pallas_call(functools.partial(kernel, seq_count, section_count), out_s...  51 us
    pallas_call x1, Pallas kernels, local(): pl.pallas_call(put, out_shape=jax.ShapeDtypeStruct(tokens.shape, tokens.d...  1.91 us

profile of v5, /device:TPU:0, one launch (start us, length us, event | category | flops | bytes accessed | tf_op | source)
XLA Modules:
  0.0 52.9 jit_solution(3030160133911235517)
XLA Ops:
  0.0 51.0 %shard_map.91.rows_ref = bf16[128,512]{1,0:T(8,128)(2,1)} custom-call(bf16[512,512]{1,0:T(8,128)(2,1)} %tokens_ref.3, f32[1,2048]{1,0:T(1,128)} %bitcast.3, f32[4,128]{1,0:T(4,128)} %bitcast.4, s32[8]{0:T(128)} %bitcast.5, s32[8]{0:T(128)} %count_ref.3, bf16[256,512]{1,0:T(8,128)(2,1)} %wq_in.1, bf16[256,128]{1,0:T(8,128)(2,1)} %wk_in.1, ...), custom_call_target="tpu_custom_call" | custom-call | tf_op jit(solution)/shard_map/pallas_call | solution.py:556
  51.0 1.9 %shard_map.92 = bf16[512,512]{1,0:T(8,128)(2,1)} custom-call(bf16[512,512]{1,0:T(8,128)(2,1)} %tokens_ref.3, bf16[128,512]{1,0:T(8,128)(2,1)} %shard_map.91.rows_ref, s32[8]{0:T(128)} %bitcast.6, s32[8]{0:T(128)} %count_ref.3), custom_call_target="tpu_custom_call" | custom-call | tf_op jit(solution)/shard_map/pallas_call | solution.py:602

commit v6 on v3

--- a/solution.py
+++ b/solution.py
@@ -526,10 +526,9 @@
     slots = rows_ref.shape[0] // BLOCK
     for slot in range(slots):
 
-        @pl.when(slot < count_ref[me])
-        def _():
-            start = pl.multiple_of(chosen_ref[me * slots + slot] * BLOCK, BLOCK)
-            mixed_ref[pl.ds(start, BLOCK), :] = rows_ref[slot * BLOCK : (slot + 1) * BLOCK, :]
+        @pl.when((slot < count_ref[me]) & (chosen_ref[me * slots + slot] == pl.program_id(0)))
+        def _():
+            mixed_ref[...] = rows_ref[slot * BLOCK : (slot + 1) * BLOCK, :]
 
 
 def local(
@@ -602,8 +601,9 @@
     return pl.pallas_call(
         put,
         out_shape=jax.ShapeDtypeStruct(tokens.shape, tokens.dtype),
-        in_specs=[vmem, vmem, smem, smem],
-        out_specs=vmem,
+        grid=(tok_rows // BLOCK,),
+        in_specs=[pl.BlockSpec((BLOCK, width), lambda step: (step, 0)), vmem, smem, smem],
+        out_specs=pl.BlockSpec((BLOCK, width), lambda step: (step, 0)),
     )(tokens, new_rows, blocks, block_counts)
 
 

time: 52.8 us -> 54.2 us (1.027)
  Pallas kernels: 52.7 us -> 54 us
    pallas_call x1, Pallas kernels: 1.92 us -> 3.28 us  [local(): pl.pallas_call(put, out_shape=jax.ShapeDtypeStruct(tokens.shape, tokens.d...]
where the time goes in v6:
time: 54.2 us; the launch traced here: 54.1 us
  Pallas kernels  54 us (100%)
    pallas_call x1, Pallas kernels, local(): pl.pallas_call(functools.partial(kernel, seq_count, section_count), out_s...  50.8 us
    pallas_call x1, Pallas kernels, local(): pl.pallas_call(put, out_shape=jax.ShapeDtypeStruct(tokens.shape, tokens.d...  3.28 us

profile of v6, /device:TPU:0, one launch (start us, length us, event | category | flops | bytes accessed | tf_op | source)
XLA Modules:
  0.0 54.1 jit_solution(3015518879593373033)
XLA Ops:
  0.0 50.8 %shard_map.91.rows_ref = bf16[128,512]{1,0:T(8,128)(2,1)} custom-call(bf16[512,512]{1,0:T(8,128)(2,1)} %tokens_ref.3, f32[1,2048]{1,0:T(1,128)} %bitcast.3, f32[4,128]{1,0:T(4,128)} %bitcast.4, s32[8]{0:T(128)} %bitcast.5, s32[8]{0:T(128)} %count_ref.3, bf16[256,512]{1,0:T(8,128)(2,1)} %wq_in.1, bf16[256,128]{1,0:T(8,128)(2,1)} %wk_in.1, ...), custom_call_target="tpu_custom_call" | custom-call | tf_op jit(solution)/shard_map/pallas_call | solution.py:555
  50.8 3.3 %shard_map.92 = bf16[512,512]{1,0:T(8,128)(2,1)} custom-call(bf16[512,512]{1,0:T(8,128)(2,1)} %tokens_ref.3, bf16[128,512]{1,0:T(8,128)(2,1)} %shard_map.91.rows_ref, s32[8]{0:T(128)} %bitcast.6, s32[8]{0:T(128)} %count_ref.3), custom_call_target="tpu_custom_call" | custom-call | tf_op jit(solution)/shard_map/pallas_call | solution.py:601
